TPU v7x, 32 devices: a whole 2x2x4 slice. The times are simulated.
32 devices in a mesh: fsdp: 8 (over z, x), context: 4 (over y, core).
Axes of the slice: x: 2, y: 2, z: 4, core: 2. Of those that a mesh axis runs over, the one named last changes fastest.
Arguments:
- tokens: bfloat16 [16, 1024, 1536], P('fsdp', 'context'), may hold values from -6 to 6
- segments: int32 [16, 1024], P('fsdp', 'context'), may hold values from 0 to 15, never falling along the last dimension, each value on 1 to 512 neighbouring positions
- w_query: bfloat16 [1536, 1536], P('fsdp'), may hold values from -0.15625 to 0.15625
- w_key: bfloat16 [1536, 768], P('fsdp'), may hold values from -0.15625 to 0.15625
- w_value: bfloat16 [1536, 768], P('fsdp'), may hold values from -0.15625 to 0.15625
- w_out: bfloat16 [1536, 1536], P('fsdp'), may hold values from -0.875 to 0.875
- w_gate: bfloat16 [1536, 4096], P('fsdp', 'context'), may hold values from -0.15625 to 0.15625
- w_up: bfloat16 [1536, 4096], P('fsdp', 'context'), may hold values from -0.15625 to 0.15625
- w_down: bfloat16 [4096, 1536], P('context', 'fsdp'), may hold values from -0.09375 to 0.09375
- gain_attn: bfloat16 [1536], P('fsdp'), may hold values from 0.5 to 1.5
- gain_mlp: bfloat16 [1536], P('fsdp'), may hold values from 0.5 to 1.5
- cotangent: bfloat16 [16, 1024, 1536], P('fsdp', 'context'), may hold values from -6 to 6
Outputs:
- output: bfloat16 [16, 1024, 1536], P('fsdp', 'context')
- grad_tokens: float32 [16, 1024, 1536], P('fsdp', 'context')
- grad_w_query: float32 [1536, 1536], P('fsdp')
- grad_w_key: float32 [1536, 768], P('fsdp')
- grad_w_value: float32 [1536, 768], P('fsdp')
- grad_w_out: float32 [1536, 1536], P('fsdp')
- grad_w_gate: float32 [1536, 4096], P('fsdp', 'context')
- grad_w_up: float32 [1536, 4096], P('fsdp', 'context')
- grad_w_down: float32 [4096, 1536], P('context', 'fsdp')
- grad_gain_attn: float32 [1536], P('fsdp')
- grad_gain_mlp: float32 [1536], P('fsdp')
Inputs may be any that keep to these rules, and one draw needn't show every extreme that they name: `segments`: in each sequence segment numbers never fall and all 16 documents appear; the longest has exactly 512 tokens.
All inputs are finite; a program needn't handle non-finite values.
Results may differ from a plain program's by a relative error of at most 0.02.
Values may be sent and summed in bfloat16 or wider, within the bound.
No kernel may reach another device: no remote copies, remote signals or barrier semaphores. Data moves between devices by JAX's collectives and lax.ppermute only.
A program may use at most 256 MiB of HBM per device.

v0:
```python
import math
import jax
import jax.numpy as jnp
from jax import lax
from jax.sharding import PartitionSpec as P

H = 16
KVH = 8
HD = 96
EPSILON = 1e-05
THETA = 100000.0


def rms_scale(values, gain):
    return values * lax.rsqrt(jnp.mean(values * values, axis=-1, keepdims=True) + EPSILON) * gain


def rotate(values, cosines, sines):
    half_width = values.shape[-1] // 2
    leading = values[..., :half_width]
    trailing = values[..., half_width:]
    return jnp.concatenate(
        [leading * cosines - trailing * sines, trailing * cosines + leading * sines], axis=-1
    )


def gated(gate_act, up_act):
    return jax.nn.silu(gate_act) * up_act


def inner(left, right):
    return jnp.einsum("ti,tj->ij", left, right, preferred_element_type=jnp.float32)


def outer_back(grad_rows, weight):
    return jnp.einsum("ti,ji->tj", grad_rows, weight, preferred_element_type=jnp.float32)


def reduce_grads(parts):
    shares = (
        lax.psum_scatter(
            parts[0].astype(jnp.bfloat16), "fsdp", scatter_dimension=0, tiled=True
        ).astype(jnp.float32),
        lax.psum_scatter(
            parts[1].astype(jnp.bfloat16), "fsdp", scatter_dimension=0, tiled=True
        ).astype(jnp.float32),
        lax.psum_scatter(
            parts[2].astype(jnp.bfloat16), "fsdp", scatter_dimension=0, tiled=True
        ).astype(jnp.float32),
        lax.psum_scatter(
            parts[3].astype(jnp.bfloat16), "fsdp", scatter_dimension=0, tiled=True
        ).astype(jnp.float32),
        lax.psum_scatter(
            parts[4].astype(jnp.bfloat16), "fsdp", scatter_dimension=0, tiled=True
        ).astype(jnp.float32),
        lax.psum_scatter(
            parts[5].astype(jnp.bfloat16), "fsdp", scatter_dimension=0, tiled=True
        ).astype(jnp.float32),
    )
    result = (
        lax.psum(shares[0].astype(jnp.bfloat16), "context").astype(jnp.float32),
        lax.psum(shares[1].astype(jnp.bfloat16), "context").astype(jnp.float32),
        lax.psum(shares[2].astype(jnp.bfloat16), "context").astype(jnp.float32),
        lax.psum(shares[3].astype(jnp.bfloat16), "context").astype(jnp.float32),
        lax.psum(shares[4].astype(jnp.bfloat16), "context").astype(jnp.float32),
        lax.psum(shares[5].astype(jnp.bfloat16), "context").astype(jnp.float32),
    )
    return result


def gather_attention(shard_query, shard_key, shard_value, shard_out, shard_gain_a, shard_gain_m):
    return (
        lax.all_gather(shard_query, "fsdp", axis=0, tiled=True),
        lax.all_gather(shard_key, "fsdp", axis=0, tiled=True),
        lax.all_gather(shard_value, "fsdp", axis=0, tiled=True),
        lax.all_gather(shard_out, "fsdp", axis=0, tiled=True),
        lax.all_gather(shard_gain_a, "fsdp", axis=0, tiled=True),
        lax.all_gather(shard_gain_m, "fsdp", axis=0, tiled=True),
    )


def gather_mlp(shard_gate, shard_up, shard_down):
    return (
        lax.all_gather(shard_gate, "fsdp", axis=0, tiled=True),
        lax.all_gather(shard_up, "fsdp", axis=0, tiled=True),
        lax.all_gather(shard_down, "fsdp", axis=1, tiled=True),
    )


def on_device(
    tokens,
    segments,
    w_query,
    w_key,
    w_value,
    w_out,
    w_gate,
    w_up,
    w_down,
    gain_attn,
    gain_mlp,
    cotangent,
):
    seq_count, tok_local, model_width = tokens.shape
    row_count = seq_count * tok_local
    groups = H // KVH
    kv_width = KVH * HD
    logit_scale = 1.0 / math.sqrt(HD)
    whole_seg = lax.all_gather(segments, "context", axis=1, tiled=True)
    length = whole_seg.shape[1]
    all_rows = seq_count * length
    offset = lax.axis_index("context") * tok_local
    key_index = jnp.arange(length, dtype=jnp.int32)
    query_index = offset + jnp.arange(tok_local, dtype=jnp.int32)
    starts = jnp.concatenate(
        [jnp.ones((seq_count, 1), dtype=bool), whole_seg[:, 1:] != whole_seg[:, :-1]], axis=1
    )
    first_index = lax.cummax(jnp.where(starts, key_index[None, :], 0), axis=1)
    positions = lax.dynamic_slice_in_dim(key_index[None, :] - first_index, offset, tok_local, 1)
    frequency = jnp.power(THETA, -(jnp.arange(HD // 2, dtype=jnp.float32) * 2.0 / HD))
    angles = positions.astype(jnp.float32)[:, :, None] * frequency[None, None, :]
    cosines = jnp.cos(angles).reshape(row_count, 1, HD // 2)
    sines = jnp.sin(angles).reshape(row_count, 1, HD // 2)
    x_flat = tokens.reshape(row_count, model_width).astype(jnp.float32)

    def masked_scores(query_sequence, k_seq, q_seg, k_seg):
        unscaled_scores = (
            jnp.einsum(
                "wxif,axf->xiwa",
                query_sequence,
                k_seq.reshape(length, KVH, HD),
                preferred_element_type=jnp.float32,
            )
            * logit_scale
        )
        allowed = (q_seg[:, None] == k_seg[None, :]) & (key_index[None, :] <= query_index[:, None])
        return jnp.where(allowed[None, None], unscaled_scores, -1e30)

    def attend(items):
        query_sequence, k_seq, v_seq, q_seg, k_seg = items
        scores = masked_scores(query_sequence, k_seq, q_seg, k_seg)
        top_score = jnp.max(scores, axis=-1, keepdims=True)
        weights = jnp.exp(scores - top_score)
        total = jnp.sum(weights, axis=-1, keepdims=True)
        attention_probabilities = (weights / total).astype(jnp.bfloat16)
        mixed_seq = jnp.einsum(
            "uvqe,eua->quva",
            attention_probabilities,
            v_seq.reshape(length, KVH, HD),
            preferred_element_type=jnp.float32,
        ).astype(jnp.bfloat16)
        return (mixed_seq, top_score + jnp.log(total))

    def forward(attn_weights, mlp_weights):
        full_query, full_key, full_value, full_out, full_gain_a, full_gain_m = attn_weights
        normed = rms_scale(x_flat, full_gain_a.astype(jnp.float32)).astype(jnp.bfloat16)
        queries = jnp.dot(normed, full_query, preferred_element_type=jnp.float32).reshape(
            row_count, H, HD
        )
        key_rows = jnp.dot(normed, full_key, preferred_element_type=jnp.float32).reshape(
            row_count, KVH, HD
        )
        value_matrix_rows = jnp.dot(normed, full_value, preferred_element_type=jnp.float32).astype(
            jnp.bfloat16
        )
        qrot = (
            rotate(queries, cosines, sines)
            .astype(jnp.bfloat16)
            .reshape(seq_count, tok_local, KVH, groups, HD)
        )
        rotary_keys = (
            rotate(key_rows, cosines, sines)
            .astype(jnp.bfloat16)
            .reshape(seq_count, tok_local, kv_width)
        )
        all_keys, all_values = (
            lax.all_gather(rotary_keys, "context", axis=1, tiled=True),
            lax.all_gather(
                value_matrix_rows.reshape(seq_count, tok_local, kv_width),
                "context",
                axis=1,
                tiled=True,
            ),
        )
        mixed, log_totals = lax.map(attend, (qrot, all_keys, all_values, segments, whole_seg))
        mixed_flat = mixed.reshape(row_count, H * HD)
        resid = x_flat + jnp.dot(mixed_flat, full_out, preferred_element_type=jnp.float32)
        full_gate, full_up, full_down = mlp_weights
        normed_two = rms_scale(resid, full_gain_m.astype(jnp.float32)).astype(jnp.bfloat16)
        all_normed_two = lax.all_gather(
            normed_two.reshape(seq_count, tok_local, model_width), "context", axis=1, tiled=True
        ).reshape(all_rows, model_width)
        gate_act = jnp.dot(all_normed_two, full_gate, preferred_element_type=jnp.float32)
        up_act = jnp.dot(all_normed_two, full_up, preferred_element_type=jnp.float32)
        hidden = gated(gate_act, up_act).astype(jnp.bfloat16)
        partial_down = jnp.dot(hidden, full_down, preferred_element_type=jnp.float32)
        down_sum = (
            lax.psum_scatter(
                partial_down.reshape(seq_count, length, model_width).astype(jnp.bfloat16),
                "context",
                scatter_dimension=1,
                tiled=True,
            )
            .astype(jnp.float32)
            .reshape(row_count, model_width)
        )
        final = resid + down_sum
        return (
            final,
            normed,
            qrot,
            all_keys,
            all_values,
            mixed,
            log_totals,
            resid,
            all_normed_two,
            gate_act,
            up_act,
            hidden,
        )

    attn_weights = gather_attention(w_query, w_key, w_value, w_out, gain_attn, gain_mlp)
    mlp_weights = gather_mlp(w_gate, w_up, w_down)
    state = forward(attn_weights, mlp_weights)
    output = state[0].astype(jnp.bfloat16).reshape(seq_count, tok_local, model_width)
    fresh = lax.optimization_barrier(
        (w_query, w_key, w_value, w_out, gain_attn, gain_mlp, w_gate, w_up, w_down, output)
    )
    attn_weights = gather_attention(fresh[0], fresh[1], fresh[2], fresh[3], fresh[4], fresh[5])
    mlp_weights = gather_mlp(fresh[6], fresh[7], fresh[8])
    state = forward(attn_weights, mlp_weights)
    (
        final,
        normed,
        qrot,
        all_keys,
        all_values,
        mixed,
        log_totals,
        resid,
        all_normed_two,
        gate_act,
        up_act,
        hidden,
    ) = state
    full_query, full_key, full_value, full_out, full_gain_a, full_gain_m = attn_weights
    full_gate, full_up, full_down = mlp_weights
    grad_out = cotangent.reshape(row_count, model_width)
    all_grad_out = lax.all_gather(cotangent, "context", axis=1, tiled=True).reshape(
        all_rows, model_width
    )
    grad_down_t = inner(all_grad_out, hidden)
    grad_hidden = outer_back(all_grad_out, full_down)
    gate_pull = jax.vjp(gated, gate_act, up_act)[1]
    grad_gate_f, grad_up_f = gate_pull(grad_hidden)
    grad_gate_act = grad_gate_f.astype(jnp.bfloat16)
    grad_up_act = grad_up_f.astype(jnp.bfloat16)
    grad_gate = inner(all_normed_two, grad_gate_act)
    grad_up = inner(all_normed_two, grad_up_act)
    part_normed_two = outer_back(grad_gate_act, full_gate) + outer_back(grad_up_act, full_up)
    grad_normed_two = lax.psum_scatter(
        part_normed_two.reshape(seq_count, length, model_width),
        "context",
        scatter_dimension=1,
        tiled=True,
    ).reshape(row_count, model_width)
    norm_pull = jax.vjp(rms_scale, resid, full_gain_m.astype(jnp.float32))[1]
    back_resid, grad_gain_m = norm_pull(grad_normed_two)
    mlp_shares = (
        lax.psum_scatter(
            grad_gate.astype(jnp.bfloat16), "fsdp", scatter_dimension=0, tiled=True
        ).astype(jnp.float32),
        lax.psum_scatter(
            grad_up.astype(jnp.bfloat16), "fsdp", scatter_dimension=0, tiled=True
        ).astype(jnp.float32),
        lax.psum_scatter(
            grad_down_t.astype(jnp.bfloat16), "fsdp", scatter_dimension=0, tiled=True
        ).astype(jnp.float32),
    )
    grad_resid = grad_out.astype(jnp.float32) + back_resid
    grad_attn = grad_resid.astype(jnp.bfloat16)
    mixed_flat = mixed.reshape(row_count, H * HD)
    grad_out_w = inner(mixed_flat, grad_attn)
    grad_mixed = (
        outer_back(grad_attn, full_out)
        .astype(jnp.bfloat16)
        .reshape(seq_count, tok_local, KVH, groups, HD)
    )

    def attend_back(items):
        query_sequence, k_seq, v_seq, q_seg, k_seg, log_total, grad_seq = items
        scores = masked_scores(query_sequence, k_seq, q_seg, k_seg)
        attention_probabilities = jnp.exp(scores - log_total)
        grad_probs = jnp.einsum(
            "wxif,axf->xiwa",
            grad_seq,
            v_seq.reshape(length, KVH, HD),
            preferred_element_type=jnp.float32,
        )
        weighted = jnp.sum(attention_probabilities * grad_probs, axis=-1, keepdims=True)
        score_gradient = (attention_probabilities * (grad_probs - weighted)).astype(jnp.bfloat16)
        grad_q = (
            jnp.einsum(
                "uvqe,eua->quva",
                score_gradient,
                k_seq.reshape(length, KVH, HD),
                preferred_element_type=jnp.float32,
            )
            * logit_scale
        )
        grad_k = (
            jnp.einsum(
                "jnbp,bjny->pjy", score_gradient, query_sequence, preferred_element_type=jnp.float32
            )
            * logit_scale
        )
        grad_v = jnp.einsum(
            "jnbp,bjny->pjy",
            attention_probabilities.astype(jnp.bfloat16),
            grad_seq,
            preferred_element_type=jnp.float32,
        )
        return (grad_q, grad_k.reshape(length, kv_width), grad_v.reshape(length, kv_width))

    grad_qrot, part_keys, part_values = lax.map(
        attend_back, (qrot, all_keys, all_values, segments, whole_seg, log_totals, grad_mixed)
    )
    grad_krot, grad_vals = (
        lax.psum_scatter(
            part_keys.astype(jnp.bfloat16), "context", scatter_dimension=1, tiled=True
        ).astype(jnp.float32),
        lax.psum_scatter(
            part_values.astype(jnp.bfloat16), "context", scatter_dimension=1, tiled=True
        ).astype(jnp.float32),
    )
    grad_queries = (
        rotate(grad_qrot.reshape(row_count, H, HD), cosines, -sines)
        .astype(jnp.bfloat16)
        .reshape(row_count, H * HD)
    )
    grad_keys = (
        rotate(grad_krot.reshape(row_count, KVH, HD), cosines, -sines)
        .astype(jnp.bfloat16)
        .reshape(row_count, kv_width)
    )
    grad_values = grad_vals.reshape(row_count, kv_width).astype(jnp.bfloat16)
    grad_query_w = inner(normed, grad_queries)
    grad_key_w = inner(normed, grad_keys)
    grad_value_w = inner(normed, grad_values)
    grad_normed = (
        outer_back(grad_queries, full_query)
        + outer_back(grad_keys, full_key)
        + outer_back(grad_values, full_value)
    )
    first_pull = jax.vjp(rms_scale, x_flat, full_gain_a.astype(jnp.float32))[1]
    back_input, grad_gain_a = first_pull(grad_normed)
    attn_grads = reduce_grads(
        (grad_query_w, grad_key_w, grad_value_w, grad_out_w, grad_gain_a, grad_gain_m)
    )
    grad_input = (grad_resid + back_input).reshape(seq_count, tok_local, model_width)
    return (
        output,
        grad_input,
        attn_grads[0],
        attn_grads[1],
        attn_grads[2],
        attn_grads[3],
        mlp_shares[0],
        mlp_shares[1],
        jnp.transpose(mlp_shares[2]),
        attn_grads[4],
        attn_grads[5],
    )


def solution(mesh):
    return jax.shard_map(
        on_device,
        mesh=mesh,
        in_specs=(
            P("fsdp", "context", None),
            P("fsdp", "context"),
            P("fsdp", None),
            P("fsdp", None),
            P("fsdp", None),
            P("fsdp", None),
            P("fsdp", "context"),
            P("fsdp", "context"),
            P("context", "fsdp"),
            P("fsdp"),
            P("fsdp"),
            P("fsdp", "context", None),
        ),
        out_specs=(
            P("fsdp", "context", None),
            P("fsdp", "context", None),
            P("fsdp", None),
            P("fsdp", None),
            P("fsdp", None),
            P("fsdp", None),
            P("fsdp", "context"),
            P("fsdp", "context"),
            P("context", "fsdp"),
            P("fsdp"),
            P("fsdp"),
        ),
        check_vma=False,
    )
```

profile of v0, /device:TPU:0, one launch (start us, length us, event | category | flops | bytes accessed | tf_op | source)
XLA Modules:
  0.0 2307.0 jit_solution(10528098979458675509)
XLA Ops:
  13.2 23.4 %all-reduce.9 = (bf16[1536]{0:T(1024)(128)(2,1)S(1)}, bf16[1536]{0:T(1024)(128)(2,1)S(1)}) all-reduce(bf16[1536]{0:T(1024)(128)(2,1)S(1)} %dynamic-update-slice, bf16[1536]{0:T(1024)(128)(2,1)S(1)} %dynamic-update-slice.1), channel_id=1, replica_groups=mesh['fsdp'=8,'context'=4] {'fsdp'}, use_global_device_ids=true, to_apply=%add.1 | all-reduce | flops 3072 | bytes 12288
  75.2 43.1 %all-gather.22.cloned.1.call-done = bf16[1536,768]{1,0:T(8,128)(2,1)} async-done(((bf16[192,768]{1,0:T(8,128)(2,1)}), bf16[1536,768]{1,0:T(8,128)(2,1)}) %all-gather.22.cloned.1.call-update) | async-done | bytes 2359312 | tf_op jit(solution)/shard_map/all_gather | solution.py:75
  124.8 74.1 %all-gather.30.cloned.1.call-done = bf16[1536,1536]{1,0:T(8,128)(2,1)} async-done(((bf16[192,1536]{1,0:T(8,128)(2,1)}), bf16[1536,1536]{1,0:T(8,128)(2,1)}) %all-gather.30.cloned.1.call-update) | async-done | bytes 4718608 | tf_op jit(solution)/shard_map/all_gather | solution.py:73
  228.0 30.9 %all-gather.24.cloned.1.call-done = bf16[2,1024,768]{1,2,0:T(8,128)(2,1)} async-done(((bf16[2,256,768]{1,2,0:T(8,128)(2,1)}), bf16[2,1024,768]{1,2,0:T(8,128)(2,1)}) %all-gather.24.cloned.1.call-update) | async-done | bytes 3145744 | tf_op jit(solution)/shard_map/all_gather | solution.py:178
  260.3 43.3 %while.39 = (s32[]{:T(128)}, bf16[2,256,8,2,96]{1,4,3,2,0:T(8,128)(2,1)}, bf16[2,1024,768]{1,2,0:T(8,128)(2,1)}, s32[2,256]{1,0:T(2,128)S(1)}, s32[2,1024]{1,0:T...) while((s32[]{:T(128)}, ...), condition=%wide.region_6.7_spmd.clone, body=%wide.region_3.6_spmd.clone.sunk | while | flops 1636959488 | bytes 45139068 | solution.py:185
  307.1 33.8 %all-gather.32.cloned.1.call-done = bf16[1536,1536]{1,0:T(8,128)(2,1)} async-done(((bf16[192,1536]{1,0:T(8,128)(2,1)}), bf16[1536,1536]{1,0:T(8,128)(2,1)}) %all-gather.32.cloned.1.call-update) | async-done | bytes 4718608 | tf_op jit(solution)/shard_map/all_gather | solution.py:76
  350.8 50.9 %all-gather.36.cloned.1.call-done = bf16[1536,1024]{1,0:T(8,128)(2,1)} async-done(((bf16[192,1024]{1,0:T(8,128)(2,1)}), bf16[1536,1024]{1,0:T(8,128)(2,1)}) %all-gather.36.cloned.1.call-update) | async-done | bytes 3145744 | tf_op jit(solution)/shard_map/all_gather | solution.py:84
  401.7 47.2 %all-gather.34.cloned.1.call-done = bf16[2,1024,1536]{2,1,0:T(8,128)(2,1)} async-done(((bf16[2,256,1536]{2,1,0:T(8,128)(2,1)}), bf16[2,1024,1536]{2,1,0:T(8,128)(2,1)}) %all-gather.34.cloned.1.call-update) | async-done | bytes 6291472 | tf_op jit(solution)/shard_map/all_gather | solution.py:190
  460.6 51.0 %all-gather.38.cloned.1.call-done = bf16[1536,1024]{1,0:T(8,128)(2,1)} async-done(((bf16[192,1024]{1,0:T(8,128)(2,1)}), bf16[1536,1024]{1,0:T(8,128)(2,1)}) %all-gather.38.cloned.1.call-update) | async-done | bytes 3145744 | tf_op jit(solution)/shard_map/all_gather | solution.py:85
  511.5 61.1 %all-gather.40.cloned.1.call-done = bf16[1024,1536]{0,1:T(8,128)(2,1)} async-done(((bf16[1024,192]{0,1:T(8,128)(2,1)}), bf16[1024,1536]{0,1:T(8,128)(2,1)}) %all-gather.40.cloned.1.call-update) | async-done | bytes 3145744 | tf_op jit(solution)/shard_map/all_gather | solution.py:86
  593.0 57.1 %reduce-scatter.14.cloned.1.call-done = bf16[2,256,1536]{2,1,0:T(8,128)(2,1)} async-done(((bf16[2,1024,1536]{2,1,0:T(8,128)(2,1)}), bf16[2,256,1536]{2,1,0:T(8,128)(2,1)}) %reduce-scatter.14.cloned.1.call-update) | async-done | bytes 1572880 | tf_op jit(solution)/shard_map/reduce_scatter | solution.py:198
  678.0 28.5 %all-gather.46.cloned.1.call-done = bf16[1536,768]{1,0:T(8,128)(2,1)} async-done(((bf16[192,768]{1,0:T(8,128)(2,1)}), bf16[1536,768]{1,0:T(8,128)(2,1)}) %all-gather.46.cloned.1.call-update) | async-done | bytes 2359312 | tf_op jit(solution)/shard_map/all_gather | solution.py:75
  713.2 46.3 %all-gather.50.cloned.1.call-done = bf16[1536,768]{1,0:T(8,128)(2,1)} async-done(((bf16[192,768]{1,0:T(8,128)(2,1)}), bf16[1536,768]{1,0:T(8,128)(2,1)}) %all-gather.50.cloned.1.call-update) | async-done | bytes 2359312 | tf_op jit(solution)/shard_map/all_gather | solution.py:74
  770.0 70.3 %all-gather.54.cloned.1.call-done = bf16[1536,1536]{1,0:T(8,128)(2,1)} async-done(((bf16[192,1536]{1,0:T(8,128)(2,1)}), bf16[1536,1536]{1,0:T(8,128)(2,1)}) %all-gather.54.cloned.1.call-update) | async-done | bytes 4718608 | tf_op jit(solution)/shard_map/all_gather | solution.py:73
  869.4 31.0 %all-gather.52.cloned.1.call-done = bf16[2,1024,768]{1,2,0:T(8,128)(2,1)} async-done(((bf16[2,256,768]{1,2,0:T(8,128)(2,1)}), bf16[2,1024,768]{1,2,0:T(8,128)(2,1)}) %all-gather.52.cloned.1.call-update) | async-done | bytes 3145744 | tf_op jit(solution)/shard_map/all_gather | solution.py:177
  901.8 57.2 %while.40 = (s32[]{:T(128)}, bf16[2,256,8,2,96]{1,4,3,2,0:T(8,128)(2,1)}, f32[2,8,2,256,1]{3,2,1,4,0:T(2,128)S(1)}, bf16[2,1024,768]{1,2,0:T(8,128)(2,1)}, s32[2...) while((s32[]{:T(128)}, ...), condition=%wide.region_12.13_spmd.clone, body=%wide.region_9.12_spmd.clone.sunk | while | flops 1662120192 | bytes 62538888 | solution.py:185
  993.2 50.3 %all-gather.62.cloned.1.call-done = bf16[1536,1024]{1,0:T(8,128)(2,1)} async-done(((bf16[192,1024]{1,0:T(8,128)(2,1)}), bf16[1536,1024]{1,0:T(8,128)(2,1)}) %all-gather.62.cloned.1.call-update) | async-done | bytes 3145744 | tf_op jit(solution)/shard_map/all_gather | solution.py:84
  1043.5 46.7 %all-gather.58.cloned.1.call-done = bf16[2,1024,1536]{2,1,0:T(8,128)(2,1)} async-done(((bf16[2,256,1536]{2,1,0:T(8,128)(2,1)}), bf16[2,1024,1536]{2,1,0:T(8,128)(2,1)}) %all-gather.58.cloned.1.call-update) | async-done | bytes 6291472 | tf_op jit(solution)/shard_map/all_gather | solution.py:190
  1101.9 51.0 %all-gather.60.cloned.1.call-done = bf16[1536,1024]{1,0:T(8,128)(2,1)} async-done(((bf16[192,1024]{1,0:T(8,128)(2,1)}), bf16[1536,1024]{1,0:T(8,128)(2,1)}) %all-gather.60.cloned.1.call-update) | async-done | bytes 3145744 | tf_op jit(solution)/shard_map/all_gather | solution.py:85
  1164.6 35.0 %all-gather.44.cloned.1.call-done = bf16[2,1024,1536]{2,1,0:T(8,128)(2,1)} async-done(((bf16[2,256,1536]{2,1,0:T(8,128)(2,1)}), bf16[2,1024,1536]{2,1,0:T(8,128)(2,1)}) %all-gather.44.cloned.1.call-update) | async-done | bytes 6291472 | tf_op jit(solution)/shard_map/all_gather | solution.py:250
  1199.6 62.9 %all-gather.42.cloned.1.call-done = bf16[1024,1536]{0,1:T(8,128)(2,1)} async-done(((bf16[1024,192]{0,1:T(8,128)(2,1)}), bf16[1024,1536]{0,1:T(8,128)(2,1)}) %all-gather.42.cloned.1.call-update) | async-done | bytes 3145744 | tf_op jit(solution)/shard_map/all_gather | solution.py:86
  1301.2 97.8 %reduce-scatter.16.cloned.1.call-done = f32[2,256,1536]{2,1,0:T(8,128)} async-done(((f32[2,1024,1536]{2,1,0:T(8,128)}), f32[2,256,1536]{2,1,0:T(8,128)}) %reduce-scatter.16.cloned.1.call-update) | async-done | bytes 3145744 | tf_op jit(solution)/shard_map/reduce_scatter | solution.py:262
  1417.6 172.9 %while.41 = (s32[]{:T(128)}, f32[2,256,8,2,96]{1,0,4,3,2:T(2,128)}, bf16[2,1024,768]{1,2,0:T(8,128)(2,1)}, bf16[2,1024,768]{2,1,0:T(8,128)(2,1)}, bf16[2,1024,76...) while((s32[]{:T(128)}, f32[2,256,8,2,96]{1,0,4,3,2:T(2,128)}, ...), condition=%wide.region_18.19_spmd.clone, body=%wide.region_16.18_spmd.clone.sunk | while | flops 4067029248 | bytes 192513344 | solution.py:326
  1467.8 32.3 %dynamic_update_slice.44 = f32[2,256,8,2,96]{1,0,4,3,2:T(2,128)} dynamic-update-slice(f32[2,256,8,2,96]{1,0,4,3,2:T(2,128)} %get-tuple-element.728, f32[1,256,8,2,96]{1,0,4,3,2:T(1,128)S(1)} %copy.145, s32[]{:T(128)S(6)} %copy.177, s32[]{:T(128)} %constant.103.clone.1..sunk, s32[]{:T(128)} %constant.103.clone.1..sunk, s32[]{:T(128)} %constant.103.clone.1..sunk, s32[]{:T(128)} %constant.103.clone.1..sunk) | dynamic-update-slice | bytes 3145732 | tf_op jit(solution)/shard_map/while/body/jit(dynamic_update_index_in_dim)/dynamic_update_slice | solution.py:326
  1554.1 32.3 %dynamic_update_slice.44 = f32[2,256,8,2,96]{1,0,4,3,2:T(2,128)} dynamic-update-slice(f32[2,256,8,2,96]{1,0,4,3,2:T(2,128)} %get-tuple-element.728, f32[1,256,8,2,96]{1,0,4,3,2:T(1,128)S(1)} %copy.145, s32[]{:T(128)S(6)} %copy.177, s32[]{:T(128)} %constant.103.clone.1..sunk, s32[]{:T(128)} %constant.103.clone.1..sunk, s32[]{:T(128)} %constant.103.clone.1..sunk, s32[]{:T(128)} %constant.103.clone.1..sunk) | dynamic-update-slice | bytes 3145732 | tf_op jit(solution)/shard_map/while/body/jit(dynamic_update_index_in_dim)/dynamic_update_slice | solution.py:326
  1673.8 73.5 %reduce-scatter.34.cloned.1.call-done = bf16[192,1024]{1,0:T(8,128)(2,1)} async-done(((bf16[1536,1024]{1,0:T(8,128)(2,1)}), bf16[192,1024]{1,0:T(8,128)(2,1)}) %reduce-scatter.34.cloned.1.call-update) | async-done | bytes 393232
  1749.8 74.8 %reduce-scatter.32.cloned.1.call-done = bf16[192,1024]{1,0:T(8,128)(2,1)} async-done(((bf16[1536,1024]{1,0:T(8,128)(2,1)}), bf16[192,1024]{1,0:T(8,128)(2,1)}) %reduce-scatter.32.cloned.1.call-update) | async-done | bytes 393232 | tf_op jit(solution)/shard_map/reduce_scatter | solution.py:274
  1826.5 75.5 %reduce-scatter.30.cloned.1.call-done = bf16[192,1024]{1,0:T(8,128)(2,1)} async-done(((bf16[1536,1024]{1,0:T(8,128)(2,1)}), bf16[192,1024]{1,0:T(8,128)(2,1)}) %reduce-scatter.30.cloned.1.call-update) | async-done | bytes 393232 | tf_op jit(solution)/shard_map/reduce_scatter | solution.py:271
  1915.2 85.3 %reduce-scatter.28.cloned.1.call-done = bf16[192,1536]{1,0:T(8,128)(2,1)} async-done(((bf16[1536,1536]{1,0:T(8,128)(2,1)}), bf16[192,1536]{1,0:T(8,128)(2,1)}) %reduce-scatter.28.cloned.1.call-update) | async-done | bytes 589840 | tf_op jit(solution)/shard_map/reduce_scatter | solution.py:50
  2000.5 99.1 %reduce-scatter.22.cloned.1.call-done = bf16[192,1536]{1,0:T(8,128)(2,1)} async-done(((bf16[1536,1536]{1,0:T(8,128)(2,1)}), bf16[192,1536]{1,0:T(8,128)(2,1)}) %reduce-scatter.22.cloned.1.call-update) | async-done | bytes 589840 | tf_op jit(solution)/shard_map/reduce_scatter | solution.py:41
  2099.7 72.7 %reduce-scatter.24.cloned.1.call-done = bf16[192,768]{1,0:T(8,128)(2,1)} async-done(((bf16[1536,768]{1,0:T(8,128)(2,1)}), bf16[192,768]{1,0:T(8,128)(2,1)}) %reduce-scatter.24.cloned.1.call-update) | async-done | bytes 294928 | tf_op jit(solution)/shard_map/reduce_scatter | solution.py:44
  2172.4 72.0 %reduce-scatter.26.cloned.1.call-done = bf16[192,768]{1,0:T(8,128)(2,1)} async-done(((bf16[1536,768]{1,0:T(8,128)(2,1)}), bf16[192,768]{1,0:T(8,128)(2,1)}) %reduce-scatter.26.cloned.1.call-update) | async-done | bytes 294928 | tf_op jit(solution)/shard_map/reduce_scatter | solution.py:47
  (385 shorter events, 679.2 us)
Async XLA Ops:
  7.9 110.3 %all-gather.22.cloned.1.call-start = ((), (), s32[]{:S(2)}) async-start(), calls=%async_computation.11 | async-start | bytes 2654208 | tf_op jit(solution)/shard_map/all_gather | solution.py:75
  8.7 190.2 %all-gather.30.cloned.1.call-start = ((), (), s32[]{:S(2)}) async-start(), calls=%async_computation.15 | async-start | bytes 5308416 | tf_op jit(solution)/shard_map/all_gather | solution.py:73
  9.4 218.6 %all-gather.28.cloned.1.call-start = ((), (), s32[]{:S(2)}) async-start(), calls=%async_computation.14 | async-start | bytes 3932160 | tf_op jit(solution)/shard_map/all_gather | solution.py:177
  74.6 184.3 %all-gather.24.cloned.1.call-start = ((), (), s32[]{:S(2)}) async-start(), calls=%async_computation.12 | async-start | bytes 3932160 | tf_op jit(solution)/shard_map/all_gather | solution.py:178
  122.5 218.4 %all-gather.32.cloned.1.call-start = ((), (), s32[]{:S(2)}) async-start(), calls=%async_computation.16 | async-start | bytes 5308416 | tf_op jit(solution)/shard_map/all_gather | solution.py:76
  123.1 278.6 %all-gather.36.cloned.1.call-start = ((), (), s32[]{:S(2)}) async-start(), calls=%async_computation.18 | async-start | bytes 3538944 | tf_op jit(solution)/shard_map/all_gather | solution.py:84
  123.8 325.0 %all-gather.34.cloned.1.call-start = ((), (), s32[]{:S(2)}) async-start(), calls=%async_computation.17 | async-start | bytes 7864320 | tf_op jit(solution)/shard_map/all_gather | solution.py:190
  348.9 162.7 %all-gather.38.cloned.1.call-start = ((), (), s32[]{:S(2)}) async-start(), calls=%async_computation.19 | async-start | bytes 3538944 | tf_op jit(solution)/shard_map/all_gather | solution.py:85
  349.6 223.1 %all-gather.40.cloned.1.call-start = ((), (), s32[]{:S(2)}) async-start(), calls=%async_computation.20 | async-start | bytes 3538944 | tf_op jit(solution)/shard_map/all_gather | solution.py:86
  350.2 299.8 %reduce-scatter.14.cloned.1.call-start = ((), (), s32[]{:S(2)}) async-start(), calls=%async_computation.21 | async-start | bytes 7864320 | tf_op jit(solution)/shard_map/reduce_scatter | solution.py:198
  592.9 113.6 %all-gather.46.cloned.1.call-start = ((), (), s32[]{:S(2)}) async-start(), calls=%async_computation.24 | async-start | bytes 2654208 | tf_op jit(solution)/shard_map/all_gather | solution.py:75
  654.0 105.6 %all-gather.50.cloned.1.call-start = ((), (), s32[]{:S(2)}) async-start(), calls=%async_computation.26 | async-start | bytes 2654208 | tf_op jit(solution)/shard_map/all_gather | solution.py:74
  654.7 185.5 %all-gather.54.cloned.1.call-start = ((), (), s32[]{:S(2)}) async-start(), calls=%async_computation.28 | async-start | bytes 5308416 | tf_op jit(solution)/shard_map/all_gather | solution.py:73
  655.3 214.1 %all-gather.48.cloned.1.call-start = ((), (), s32[]{:S(2)}) async-start(), calls=%async_computation.25 | async-start | bytes 3932160 | tf_op jit(solution)/shard_map/all_gather | solution.py:178
  712.7 187.7 %all-gather.52.cloned.1.call-start = ((), (), s32[]{:S(2)}) async-start(), calls=%async_computation.27 | async-start | bytes 3932160 | tf_op jit(solution)/shard_map/all_gather | solution.py:177
  768.5 214.1 %all-gather.56.cloned.1.call-start = ((), (), s32[]{:S(2)}) async-start(), calls=%async_computation.29 | async-start | bytes 5308416 | tf_op jit(solution)/shard_map/all_gather | solution.py:76
  769.1 274.4 %all-gather.62.cloned.1.call-start = ((), (), s32[]{:S(2)}) async-start(), calls=%async_computation.32 | async-start | bytes 3538944 | tf_op jit(solution)/shard_map/all_gather | solution.py:84
  769.8 320.4 %all-gather.58.cloned.1.call-start = ((), (), s32[]{:S(2)}) async-start(), calls=%async_computation.30 | async-start | bytes 7864320 | tf_op jit(solution)/shard_map/all_gather | solution.py:190
  991.1 161.8 %all-gather.60.cloned.1.call-start = ((), (), s32[]{:S(2)}) async-start(), calls=%async_computation.31 | async-start | bytes 3538944 | tf_op jit(solution)/shard_map/all_gather | solution.py:85
  991.7 207.9 %all-gather.44.cloned.1.call-start = ((), (), s32[]{:S(2)}) async-start(), calls=%async_computation.23 | async-start | bytes 7864320 | tf_op jit(solution)/shard_map/all_gather | solution.py:250
  992.4 270.1 %all-gather.42.cloned.1.call-start = ((), (), s32[]{:S(2)}) async-start(), calls=%async_computation.22 | async-start | bytes 3538944 | tf_op jit(solution)/shard_map/all_gather | solution.py:86
  993.2 405.8 %reduce-scatter.16.cloned.1.call-start = ((), (), s32[]{:S(2)}) async-start(), calls=%async_computation.33 | async-start | bytes 15728640 | tf_op jit(solution)/shard_map/reduce_scatter | solution.py:262
  1301.1 350.5 %reduce-scatter.18.cloned.1.call-start = ((), (), s32[]{:S(2)}) async-start(), calls=%async_computation.34 | async-start | bytes 3932160 | tf_op jit(solution)/shard_map/reduce_scatter | solution.py:330
  1590.5 78.6 %reduce-scatter.20.cloned.1.call-start = ((), (), s32[]{:S(2)}) async-start(), calls=%async_computation.35 | async-start | bytes 3932160 | tf_op jit(solution)/shard_map/reduce_scatter | solution.py:333
  1591.3 156.0 %reduce-scatter.34.cloned.1.call-start = ((), (), s32[]{:S(2)}) async-start(), calls=%async_computation.42 | async-start | bytes 3538944
  1610.2 214.4 %reduce-scatter.32.cloned.1.call-start = ((), (), s32[]{:S(2)}) async-start(), calls=%async_computation.41 | async-start | bytes 3538944 | tf_op jit(solution)/shard_map/reduce_scatter | solution.py:274
  1621.5 280.5 %reduce-scatter.30.cloned.1.call-start = ((), (), s32[]{:S(2)}) async-start(), calls=%async_computation.40 | async-start | bytes 3538944 | tf_op jit(solution)/shard_map/reduce_scatter | solution.py:271
  1633.0 367.6 %reduce-scatter.28.cloned.1.call-start = ((), (), s32[]{:S(2)}) async-start(), calls=%async_computation.39 | async-start | bytes 5308416 | tf_op jit(solution)/shard_map/reduce_scatter | solution.py:50
  1640.6 459.1 %reduce-scatter.22.cloned.1.call-start = ((), (), s32[]{:S(2)}) async-start(), calls=%async_computation.36 | async-start | bytes 5308416 | tf_op jit(solution)/shard_map/reduce_scatter | solution.py:41
  1651.5 520.9 %reduce-scatter.24.cloned.1.call-start = ((), (), s32[]{:S(2)}) async-start(), calls=%async_computation.37 | async-start | bytes 2654208 | tf_op jit(solution)/shard_map/reduce_scatter | solution.py:44
  1659.0 585.4 %reduce-scatter.26.cloned.1.call-start = ((), (), s32[]{:S(2)}) async-start(), calls=%async_computation.38 | async-start | bytes 2654208 | tf_op jit(solution)/shard_map/reduce_scatter | solution.py:47
  1673.1 619.8 %all-reduce.14.cloned.1.call-start = ((), (), s32[]{:S(2)}) async-start(), calls=%async_computation.43 | async-start | bytes 3538944 | tf_op jit(solution)/shard_map/psum | solution.py:61
  (59 other events, 2005.2 us)
Sparse Core Ops, SparseCore 0:
  10.2 55.0 all-gather.25
  67.5 50.7 all-gather.21
  120.4 78.4 all-gather.29
  200.9 27.0 all-gather.27
  230.0 28.9 all-gather.23
  261.0 79.8 all-gather.31
  343.1 58.5 all-gather.35
  403.8 44.9 all-gather.33
  451.1 60.4 all-gather.37
  513.6 59.0 all-gather.39
  593.0 56.9 reduce-scatter.13
  654.1 52.3 all-gather.45
  708.9 50.6 all-gather.49
  761.8 78.4 all-gather.53
  871.5 28.9 all-gather.51
  902.7 79.8 all-gather.55
  984.9 58.5 all-gather.61
  1045.2 44.9 all-gather.57
  1092.5 60.4 all-gather.59
  1154.6 45.0 all-gather.43
  1202.1 60.4 all-gather.41
  1301.2 97.6 reduce-scatter.15
  1590.7 37.9 reduce-scatter.17
  1631.2 37.9 reduce-scatter.19
  1673.0 74.2 reduce-scatter.33
  1751.2 73.3 reduce-scatter.31
  1828.6 73.3 reduce-scatter.29
  1906.1 94.4 reduce-scatter.27
  2004.5 95.1 reduce-scatter.21
  2103.6 68.7 reduce-scatter.23
  2176.3 68.0 reduce-scatter.25
  2247.1 45.7 all-reduce.13
  (1 shorter events, 27.0 us)
where the time goes:
time: 2320 us; the launch traced here: 2310 us
  waiting for transfers between devices  1630 us (70%)
  matrix products  333 us (14%)
  local copies, waits for them, and re-layouts  171 us (7%)
  other arithmetic  81.4 us (4%)
  blocking collectives  75.4 us (3%)
    all_gather x2, waiting for transfers between devices, gather_attention(): lax.all_gather(shard_query, 'fsdp', axis=0, tiled=True)  144 us
    all_gather x2, waiting for transfers between devices, gather_mlp(): lax.all_gather(shard_down, 'fsdp', axis=1, tiled=True)  124 us
    all_gather x2, waiting for transfers between devices, gather_mlp(): lax.all_gather(shard_up, 'fsdp', axis=0, tiled=True)  102 us
    all_gather x2, waiting for transfers between devices, gather_mlp(): lax.all_gather(shard_gate, 'fsdp', axis=0, tiled=True)  101 us
    reduce_scatter x1, waiting for transfers between devices, reduce_grads(): lax.psum_scatter(parts[0].astype(jnp.bfloat16), 'fsdp', scatter_dimension...  99.1 us
    reduce_scatter x1, waiting for transfers between devices, on_device(): lax.psum_scatter(part_normed_two.reshape(seq_count, length, model_width),...  97.8 us
    all_gather x2, waiting for transfers between devices, forward(): lax.all_gather(normed_two.reshape(seq_count, tok_local, model_width), 'co...  93.9 us
    reduce_scatter x1, waiting for transfers between devices, reduce_grads(): lax.psum_scatter(parts[3].astype(jnp.bfloat16), 'fsdp', scatter_dimension...  85.3 us
  transfers between devices with their start and end apart: 33, of which 32 were waited for; matrix products, arithmetic and copies ran while one was open for 14% of the time, Pallas kernels for 0%

commit v1 on v0

--- a/solution.py
+++ b/solution.py
@@ -1,14 +1,45 @@
+import functools
 import math
 import jax
 import jax.numpy as jnp
 from jax import lax
 from jax.sharding import PartitionSpec as P
+from jax.lax import axis_index, axis_size, ppermute
 
 H = 16
 KVH = 8
 HD = 96
 EPSILON = 1e-05
 THETA = 100000.0
+
+
+def hold_units(shard_in, join_dim):
+    shard_in = jnp.moveaxis(shard_in, 0, join_dim)
+    part_now = shard_in.shape
+    return shard_in.reshape(
+        *part_now[:join_dim], part_now[join_dim] * part_now[join_dim + 1], *part_now[join_dim + 2 :]
+    )
+
+
+def arrange_threads(inp, comm_axis, dim_no):
+    devs = axis_size(comm_axis)
+    frames = [(at, (at + 1) % devs) for at in range(devs)]
+    state_now, mixed_arr = ([], [])
+    made = [(no, j) for j, no in frames]
+    for s in range(devs - 1):
+        if s % 2 == 0:
+            state_now.append(ppermute(state_now[-1] if state_now else inp, comm_axis, frames))
+        else:
+            mixed_arr.append(ppermute(mixed_arr[-1] if mixed_arr else inp, comm_axis, made))
+    front = jnp.stack([*state_now[::-1], inp, *mixed_arr], axis=0)
+    f_next = axis_index(comm_axis)
+    r2 = len(state_now)
+    formed = f_next - r2
+    front = front[(jnp.arange(devs) - formed) % devs]
+    return hold_units(front, dim_no)
+
+
+track_map = functools.partial(arrange_threads, comm_axis="fsdp", dim_no=0)
 
 
 def rms_scale(values, gain):
@@ -72,7 +103,7 @@
     return (
         lax.all_gather(shard_query, "fsdp", axis=0, tiled=True),
         lax.all_gather(shard_key, "fsdp", axis=0, tiled=True),
-        lax.all_gather(shard_value, "fsdp", axis=0, tiled=True),
+        track_map(shard_value),
         lax.all_gather(shard_out, "fsdp", axis=0, tiled=True),
         lax.all_gather(shard_gain_a, "fsdp", axis=0, tiled=True),
         lax.all_gather(shard_gain_m, "fsdp", axis=0, tiled=True),

time: 2320 us -> 2250 us (0.970)
  waiting for transfers between devices: 1630 us -> 1520 us
  starting transfers between devices: 2.31 us -> 28 us
    all_gather x2 -> x0, waiting for transfers between devices: 71.6 us -> none  [gather_attention(): lax.all_gather(shard_value, 'fsdp', axis=0, tiled=True)]
    ppermute x0 -> x14, waiting for transfers between devices: none -> 71.1 us  [the longest x8 45.5 us: arrange_threads(): ppermute(state_now[-1] if state_now else inp, comm_axis, frames)]
    all_gather x2, waiting for transfers between devices: 63.9 us -> 0.02 us  [gather_attention(): lax.all_gather(shard_key, 'fsdp', axis=0, tiled=True)]
    all_gather x2, waiting for transfers between devices: 144 us -> 105 us  [gather_attention(): lax.all_gather(shard_query, 'fsdp', axis=0, tiled=True)]
    ppermute x0 -> x14, starting transfers between devices: none -> 25.8 us  [the longest x6 18.8 us: arrange_threads(): ppermute(mixed_arr[-1] if mixed_arr else inp, comm_axis, made)]
    unnamed x34 -> x32, waiting for transfers between devices: 82.6 us -> 81.1 us
  transfers between devices with their start and end apart: 33 -> 45, of which waited for: 32 -> 36; matrix products, arithmetic and copies ran while one was open for 14% -> 15% of each run, Pallas kernels for 0% -> 0%
where the time goes in v1:
time: 2250 us; the launch traced here: 2240 us
  waiting for transfers between devices  1520 us (68%)
  matrix products  333 us (15%)
  local copies, waits for them, and re-layouts  180 us (8%)
  other arithmetic  82.3 us (4%)
  blocking collectives  75.5 us (3%)
  starting transfers between devices  28 us (1%)
    all_gather x2, waiting for transfers between devices, gather_mlp(): lax.all_gather(shard_down, 'fsdp', axis=1, tiled=True)  124 us
    all_gather x2, waiting for transfers between devices, gather_attention(): lax.all_gather(shard_query, 'fsdp', axis=0, tiled=True)  105 us
    all_gather x2, waiting for transfers between devices, gather_mlp(): lax.all_gather(shard_up, 'fsdp', axis=0, tiled=True)  102 us
    all_gather x2, waiting for transfers between devices, gather_mlp(): lax.all_gather(shard_gate, 'fsdp', axis=0, tiled=True)  101 us
    reduce_scatter x1, waiting for transfers between devices, reduce_grads(): lax.psum_scatter(parts[0].astype(jnp.bfloat16), 'fsdp', scatter_dimension...  99.1 us
    reduce_scatter x1, waiting for transfers between devices, on_device(): lax.psum_scatter(part_normed_two.reshape(seq_count, length, model_width),...  97.8 us
    all_gather x2, waiting for transfers between devices, forward(): lax.all_gather(normed_two.reshape(seq_count, tok_local, model_width), 'co...  93.7 us
    reduce_scatter x1, waiting for transfers between devices, reduce_grads(): lax.psum_scatter(parts[3].astype(jnp.bfloat16), 'fsdp', scatter_dimension...  85.2 us
  transfers between devices with their start and end apart: 45, of which 36 were waited for; matrix products, arithmetic and copies ran while one was open for 15% of the time, Pallas kernels for 0%

profile of v1, /device:TPU:0, one launch (start us, length us, event | category | flops | bytes accessed | tf_op | source)
XLA Modules:
  0.0 2237.7 jit_solution(1122833712052298900)
XLA Ops:
  45.2 22.2 all-reduce.9
  114.1 49.4 %all-gather.26.cloned.1.call-done = bf16[1536,1536]{1,0:T(8,128)(2,1)} async-done(((bf16[192,1536]{1,0:T(8,128)(2,1)}), bf16[1536,1536]{1,0:T(8,128)(2,1)}) %all-gather.26.cloned.1.call-update) | async-done | bytes 4718608 | tf_op jit(solution)/shard_map/all_gather | solution.py:104
  192.7 30.9 %all-gather.24.cloned.1.call-done = bf16[2,1024,768]{1,2,0:T(8,128)(2,1)} async-done(((bf16[2,256,768]{1,2,0:T(8,128)(2,1)}), bf16[2,1024,768]{1,2,0:T(8,128)(2,1)}) %all-gather.24.cloned.1.call-update) | async-done | bytes 3145744 | tf_op jit(solution)/shard_map/all_gather | solution.py:208
  225.0 43.3 %while.39 = (s32[]{:T(128)}, bf16[2,256,8,2,96]{1,4,3,2,0:T(8,128)(2,1)}, bf16[2,1024,768]{1,2,0:T(8,128)(2,1)}, s32[2,256]{1,0:T(2,128)S(1)}, s32[2,1024]{1,0:T...) while((s32[]{:T(128)}, ...), condition=%wide.region_6.7_spmd.clone, body=%wide.region_3.6_spmd.clone.sunk | while | flops 1636959488 | bytes 45139068 | solution.py:216
  271.8 33.8 %all-gather.28.cloned.1.call-done = bf16[1536,1536]{1,0:T(8,128)(2,1)} async-done(((bf16[192,1536]{1,0:T(8,128)(2,1)}), bf16[1536,1536]{1,0:T(8,128)(2,1)}) %all-gather.28.cloned.1.call-update) | async-done | bytes 4718608 | tf_op jit(solution)/shard_map/all_gather | solution.py:107
  315.7 50.6 %all-gather.32.cloned.1.call-done = bf16[1536,1024]{1,0:T(8,128)(2,1)} async-done(((bf16[192,1024]{1,0:T(8,128)(2,1)}), bf16[1536,1024]{1,0:T(8,128)(2,1)}) %all-gather.32.cloned.1.call-update) | async-done | bytes 3145744 | tf_op jit(solution)/shard_map/all_gather | solution.py:115
  366.3 47.2 %all-gather.30.cloned.1.call-done = bf16[2,1024,1536]{2,1,0:T(8,128)(2,1)} async-done(((bf16[2,256,1536]{2,1,0:T(8,128)(2,1)}), bf16[2,1024,1536]{2,1,0:T(8,128)(2,1)}) %all-gather.30.cloned.1.call-update) | async-done | bytes 6291472 | tf_op jit(solution)/shard_map/all_gather | solution.py:221
  425.2 51.0 %all-gather.34.cloned.1.call-done = bf16[1536,1024]{1,0:T(8,128)(2,1)} async-done(((bf16[192,1024]{1,0:T(8,128)(2,1)}), bf16[1536,1024]{1,0:T(8,128)(2,1)}) %all-gather.34.cloned.1.call-update) | async-done | bytes 3145744 | tf_op jit(solution)/shard_map/all_gather | solution.py:116
  476.1 61.3 %all-gather.36.cloned.1.call-done = bf16[1024,1536]{0,1:T(8,128)(2,1)} async-done(((bf16[1024,192]{0,1:T(8,128)(2,1)}), bf16[1024,1536]{0,1:T(8,128)(2,1)}) %all-gather.36.cloned.1.call-update) | async-done | bytes 3145744 | tf_op jit(solution)/shard_map/all_gather | solution.py:117
  537.4 20.2 convolution_convert_fusion.2
  557.7 57.0 %reduce-scatter.14.cloned.1.call-done = bf16[2,256,1536]{2,1,0:T(8,128)(2,1)} async-done(((bf16[2,1024,1536]{2,1,0:T(8,128)(2,1)}), bf16[2,256,1536]{2,1,0:T(8,128)(2,1)}) %reduce-scatter.14.cloned.1.call-update) | async-done | bytes 1572880 | tf_op jit(solution)/shard_map/reduce_scatter | solution.py:229
  648.8 23.0 %all-reduce.8 = (bf16[1536]{0:T(1024)(128)(2,1)S(1)}, bf16[1536]{0:T(1024)(128)(2,1)S(1)}) all-reduce(bf16[1536]{0:T(1024)(128)(2,1)S(1)} %dynamic-update-slice.2, bf16[1536]{0:T(1024)(128)(2,1)S(1)} %dynamic-update-slice.3), channel_id=1, replica_groups=mesh['fsdp'=8,'context'=4] {'fsdp'}, use_global_device_ids=true, to_apply=%add.3 | all-reduce | flops 3072 | bytes 12288
  714.9 55.8 %all-gather.48.cloned.1.call-done = bf16[1536,1536]{1,0:T(8,128)(2,1)} async-done(((bf16[192,1536]{1,0:T(8,128)(2,1)}), bf16[1536,1536]{1,0:T(8,128)(2,1)}) %all-gather.48.cloned.1.call-update) | async-done | bytes 4718608 | tf_op jit(solution)/shard_map/all_gather | solution.py:104
  800.1 31.0 %all-gather.46.cloned.1.call-done = bf16[2,1024,768]{1,2,0:T(8,128)(2,1)} async-done(((bf16[2,256,768]{1,2,0:T(8,128)(2,1)}), bf16[2,1024,768]{1,2,0:T(8,128)(2,1)}) %all-gather.46.cloned.1.call-update) | async-done | bytes 3145744 | tf_op jit(solution)/shard_map/all_gather | solution.py:208
  832.4 57.1 %while.40 = (s32[]{:T(128)}, bf16[2,256,8,2,96]{1,4,3,2,0:T(8,128)(2,1)}, f32[2,8,2,256,1]{3,2,1,4,0:T(2,128)S(1)}, bf16[2,1024,768]{1,2,0:T(8,128)(2,1)}, s32[2...) while((s32[]{:T(128)}, ...), condition=%wide.region_12.13_spmd.clone, body=%wide.region_9.12_spmd.clone.sunk | while | flops 1662120192 | bytes 62538888 | solution.py:216
  923.7 50.5 %all-gather.56.cloned.1.call-done = bf16[1536,1024]{1,0:T(8,128)(2,1)} async-done(((bf16[192,1024]{1,0:T(8,128)(2,1)}), bf16[1536,1024]{1,0:T(8,128)(2,1)}) %all-gather.56.cloned.1.call-update) | async-done | bytes 3145744 | tf_op jit(solution)/shard_map/all_gather | solution.py:115
  974.2 46.5 %all-gather.52.cloned.1.call-done = bf16[2,1024,1536]{2,1,0:T(8,128)(2,1)} async-done(((bf16[2,256,1536]{2,1,0:T(8,128)(2,1)}), bf16[2,1024,1536]{2,1,0:T(8,128)(2,1)}) %all-gather.52.cloned.1.call-update) | async-done | bytes 6291472 | tf_op jit(solution)/shard_map/all_gather | solution.py:221
  1032.4 51.0 %all-gather.54.cloned.1.call-done = bf16[1536,1024]{1,0:T(8,128)(2,1)} async-done(((bf16[192,1024]{1,0:T(8,128)(2,1)}), bf16[1536,1024]{1,0:T(8,128)(2,1)}) %all-gather.54.cloned.1.call-update) | async-done | bytes 3145744 | tf_op jit(solution)/shard_map/all_gather | solution.py:116
  1095.1 35.0 %all-gather.40.cloned.1.call-done = bf16[2,1024,1536]{2,1,0:T(8,128)(2,1)} async-done(((bf16[2,256,1536]{2,1,0:T(8,128)(2,1)}), bf16[2,1024,1536]{2,1,0:T(8,128)(2,1)}) %all-gather.40.cloned.1.call-update) | async-done | bytes 6291472 | tf_op jit(solution)/shard_map/all_gather | solution.py:281
  1130.1 62.7 %all-gather.38.cloned.1.call-done = bf16[1024,1536]{0,1:T(8,128)(2,1)} async-done(((bf16[1024,192]{0,1:T(8,128)(2,1)}), bf16[1024,1536]{0,1:T(8,128)(2,1)}) %all-gather.38.cloned.1.call-update) | async-done | bytes 3145744 | tf_op jit(solution)/shard_map/all_gather | solution.py:117
  1231.6 97.8 %reduce-scatter.16.cloned.1.call-done = f32[2,256,1536]{2,1,0:T(8,128)} async-done(((f32[2,1024,1536]{2,1,0:T(8,128)}), f32[2,256,1536]{2,1,0:T(8,128)}) %reduce-scatter.16.cloned.1.call-update) | async-done | bytes 3145744 | tf_op jit(solution)/shard_map/reduce_scatter | solution.py:293
  1348.0 172.9 %while.41 = (s32[]{:T(128)}, f32[2,256,8,2,96]{1,0,4,3,2:T(2,128)}, bf16[2,1024,768]{1,2,0:T(8,128)(2,1)}, bf16[2,1024,768]{2,1,0:T(8,128)(2,1)}, bf16[2,1024,76...) while((s32[]{:T(128)}, f32[2,256,8,2,96]{1,0,4,3,2:T(2,128)}, ...), condition=%wide.region_18.19_spmd.clone, body=%wide.region_16.18_spmd.clone.sunk | while | flops 4067029248 | bytes 192513344 | solution.py:357
  1398.2 32.3 %dynamic_update_slice.44 = f32[2,256,8,2,96]{1,0,4,3,2:T(2,128)} dynamic-update-slice(f32[2,256,8,2,96]{1,0,4,3,2:T(2,128)} %get-tuple-element.728, f32[1,256,8,2,96]{1,0,4,3,2:T(1,128)S(1)} %copy.145, s32[]{:T(128)S(6)} %copy.191, s32[]{:T(128)} %constant.125.clone.1..sunk, s32[]{:T(128)} %constant.125.clone.1..sunk, s32[]{:T(128)} %constant.125.clone.1..sunk, s32[]{:T(128)} %constant.125.clone.1..sunk) | dynamic-update-slice | bytes 3145732 | tf_op jit(solution)/shard_map/while/body/jit(dynamic_update_index_in_dim)/dynamic_update_slice | solution.py:357
  1484.5 32.3 %dynamic_update_slice.44 = f32[2,256,8,2,96]{1,0,4,3,2:T(2,128)} dynamic-update-slice(f32[2,256,8,2,96]{1,0,4,3,2:T(2,128)} %get-tuple-element.728, f32[1,256,8,2,96]{1,0,4,3,2:T(1,128)S(1)} %copy.145, s32[]{:T(128)S(6)} %copy.191, s32[]{:T(128)} %constant.125.clone.1..sunk, s32[]{:T(128)} %constant.125.clone.1..sunk, s32[]{:T(128)} %constant.125.clone.1..sunk, s32[]{:T(128)} %constant.125.clone.1..sunk) | dynamic-update-slice | bytes 3145732 | tf_op jit(solution)/shard_map/while/body/jit(dynamic_update_index_in_dim)/dynamic_update_slice | solution.py:357
  1604.3 73.5 %reduce-scatter.34.cloned.1.call-done = bf16[192,1024]{1,0:T(8,128)(2,1)} async-done(((bf16[1536,1024]{1,0:T(8,128)(2,1)}), bf16[192,1024]{1,0:T(8,128)(2,1)}) %reduce-scatter.34.cloned.1.call-update) | async-done | bytes 393232
  1680.3 75.3 %reduce-scatter.32.cloned.1.call-done = bf16[192,1024]{1,0:T(8,128)(2,1)} async-done(((bf16[1536,1024]{1,0:T(8,128)(2,1)}), bf16[192,1024]{1,0:T(8,128)(2,1)}) %reduce-scatter.32.cloned.1.call-update) | async-done | bytes 393232 | tf_op jit(solution)/shard_map/reduce_scatter | solution.py:305
  1757.6 75.3 %reduce-scatter.30.cloned.1.call-done = bf16[192,1024]{1,0:T(8,128)(2,1)} async-done(((bf16[1536,1024]{1,0:T(8,128)(2,1)}), bf16[192,1024]{1,0:T(8,128)(2,1)}) %reduce-scatter.30.cloned.1.call-update) | async-done | bytes 393232 | tf_op jit(solution)/shard_map/reduce_scatter | solution.py:302
  1846.1 85.2 %reduce-scatter.28.cloned.1.call-done = bf16[192,1536]{1,0:T(8,128)(2,1)} async-done(((bf16[1536,1536]{1,0:T(8,128)(2,1)}), bf16[192,1536]{1,0:T(8,128)(2,1)}) %reduce-scatter.28.cloned.1.call-update) | async-done | bytes 589840 | tf_op jit(solution)/shard_map/reduce_scatter | solution.py:81
  1931.3 99.1 %reduce-scatter.22.cloned.1.call-done = bf16[192,1536]{1,0:T(8,128)(2,1)} async-done(((bf16[1536,1536]{1,0:T(8,128)(2,1)}), bf16[192,1536]{1,0:T(8,128)(2,1)}) %reduce-scatter.22.cloned.1.call-update) | async-done | bytes 589840 | tf_op jit(solution)/shard_map/reduce_scatter | solution.py:72
  2030.4 72.7 %reduce-scatter.24.cloned.1.call-done = bf16[192,768]{1,0:T(8,128)(2,1)} async-done(((bf16[1536,768]{1,0:T(8,128)(2,1)}), bf16[192,768]{1,0:T(8,128)(2,1)}) %reduce-scatter.24.cloned.1.call-update) | async-done | bytes 294928 | tf_op jit(solution)/shard_map/reduce_scatter | solution.py:75
  2103.1 71.9 %reduce-scatter.26.cloned.1.call-done = bf16[192,768]{1,0:T(8,128)(2,1)} async-done(((bf16[1536,768]{1,0:T(8,128)(2,1)}), bf16[192,768]{1,0:T(8,128)(2,1)}) %reduce-scatter.26.cloned.1.call-update) | async-done | bytes 294928 | tf_op jit(solution)/shard_map/reduce_scatter | solution.py:78
  2175.0 19.5 all-reduce.7
  (429 shorter events, 705.7 us)
Async XLA Ops:
  7.2 95.8 %all-gather.22.cloned.1.call-start = ((), (), s32[]{:S(2)}) async-start(), calls=%async_computation.12 | async-start | bytes 2654208 | tf_op jit(solution)/shard_map/all_gather | solution.py:105
  7.9 155.6 %all-gather.26.cloned.1.call-start = ((), (), s32[]{:S(2)}) async-start(), calls=%async_computation.14 | async-start | bytes 5308416 | tf_op jit(solution)/shard_map/all_gather | solution.py:104
  8.7 184.0 %all-gather.20.cloned.1.call-start = ((), (), s32[]{:S(2)}) async-start(), calls=%async_computation.11 | async-start | bytes 3932160 | tf_op jit(solution)/shard_map/all_gather | solution.py:209
  22.0 46.0 %collective-permute-start.4 = (bf16[192,768]{1,0:T(8,128)(2,1)}, bf16[192,768]{1,0:T(8,128)(2,1)S(1)}, u32[]{:S(2)}, u32[]{:S(2)}) collective-permute-start(bf16[192,768]{1,0:T(8,128)(2,1)} %param.22), channel_id=1, source_target_pairs={{4,0},{8,4},{12,8},{16,12},{20,16},{24,20},{28,24},{0,28},{5,1},{9... | collective-permute-start | bytes 884744 | tf_op jit(solution)/shard_map/ppermute | solution.py:33
  95.2 128.4 %all-gather.24.cloned.1.call-start = ((), (), s32[]{:S(2)}) async-start(), calls=%async_computation.13 | async-start | bytes 3932160 | tf_op jit(solution)/shard_map/all_gather | solution.py:208
  112.0 193.7 %all-gather.28.cloned.1.call-start = ((), (), s32[]{:S(2)}) async-start(), calls=%async_computation.15 | async-start | bytes 5308416 | tf_op jit(solution)/shard_map/all_gather | solution.py:107
  112.5 253.7 %all-gather.32.cloned.1.call-start = ((), (), s32[]{:S(2)}) async-start(), calls=%async_computation.17 | async-start | bytes 3538944 | tf_op jit(solution)/shard_map/all_gather | solution.py:115
  113.1 300.3 %all-gather.30.cloned.1.call-start = ((), (), s32[]{:S(2)}) async-start(), calls=%async_computation.16 | async-start | bytes 7864320 | tf_op jit(solution)/shard_map/all_gather | solution.py:221
  313.6 162.5 %all-gather.34.cloned.1.call-start = ((), (), s32[]{:S(2)}) async-start(), calls=%async_computation.18 | async-start | bytes 3538944 | tf_op jit(solution)/shard_map/all_gather | solution.py:116
  314.4 223.1 %all-gather.36.cloned.1.call-start = ((), (), s32[]{:S(2)}) async-start(), calls=%async_computation.19 | async-start | bytes 3538944 | tf_op jit(solution)/shard_map/all_gather | solution.py:117
  315.1 299.6 %reduce-scatter.14.cloned.1.call-start = ((), (), s32[]{:S(2)}) async-start(), calls=%async_computation.20 | async-start | bytes 7864320 | tf_op jit(solution)/shard_map/reduce_scatter | solution.py:229
  557.7 146.8 %all-gather.44.cloned.1.call-start = ((), (), s32[]{:S(2)}) async-start(), calls=%async_computation.24 | async-start | bytes 2654208 | tf_op jit(solution)/shard_map/all_gather | solution.py:105
  618.7 152.0 %all-gather.48.cloned.1.call-start = ((), (), s32[]{:S(2)}) async-start(), calls=%async_computation.26 | async-start | bytes 5308416 | tf_op jit(solution)/shard_map/all_gather | solution.py:104
  619.3 180.8 %all-gather.42.cloned.1.call-start = ((), (), s32[]{:S(2)}) async-start(), calls=%async_computation.23 | async-start | bytes 3932160 | tf_op jit(solution)/shard_map/all_gather | solution.py:209
  704.3 126.8 %all-gather.46.cloned.1.call-start = ((), (), s32[]{:S(2)}) async-start(), calls=%async_computation.25 | async-start | bytes 3932160 | tf_op jit(solution)/shard_map/all_gather | solution.py:208
  713.6 199.7 %all-gather.50.cloned.1.call-start = ((), (), s32[]{:S(2)}) async-start(), calls=%async_computation.27 | async-start | bytes 5308416 | tf_op jit(solution)/shard_map/all_gather | solution.py:107
  714.2 260.0 %all-gather.56.cloned.1.call-start = ((), (), s32[]{:S(2)}) async-start(), calls=%async_computation.30 | async-start | bytes 3538944 | tf_op jit(solution)/shard_map/all_gather | solution.py:115
  714.9 305.8 %all-gather.52.cloned.1.call-start = ((), (), s32[]{:S(2)}) async-start(), calls=%async_computation.28 | async-start | bytes 7864320 | tf_op jit(solution)/shard_map/all_gather | solution.py:221
  921.7 161.7 %all-gather.54.cloned.1.call-start = ((), (), s32[]{:S(2)}) async-start(), calls=%async_computation.29 | async-start | bytes 3538944 | tf_op jit(solution)/shard_map/all_gather | solution.py:116
  922.3 207.8 %all-gather.40.cloned.1.call-start = ((), (), s32[]{:S(2)}) async-start(), calls=%async_computation.22 | async-start | bytes 7864320 | tf_op jit(solution)/shard_map/all_gather | solution.py:281
  923.0 269.8 %all-gather.38.cloned.1.call-start = ((), (), s32[]{:S(2)}) async-start(), calls=%async_computation.21 | async-start | bytes 3538944 | tf_op jit(solution)/shard_map/all_gather | solution.py:117
  923.6 405.8 %reduce-scatter.16.cloned.1.call-start = ((), (), s32[]{:S(2)}) async-start(), calls=%async_computation.31 | async-start | bytes 15728640 | tf_op jit(solution)/shard_map/reduce_scatter | solution.py:293
  1231.6 350.4 %reduce-scatter.18.cloned.1.call-start = ((), (), s32[]{:S(2)}) async-start(), calls=%async_computation.32 | async-start | bytes 3932160 | tf_op jit(solution)/shard_map/reduce_scatter | solution.py:361
  1520.9 78.6 %reduce-scatter.20.cloned.1.call-start = ((), (), s32[]{:S(2)}) async-start(), calls=%async_computation.33 | async-start | bytes 3932160 | tf_op jit(solution)/shard_map/reduce_scatter | solution.py:364
  1521.7 156.2 %reduce-scatter.34.cloned.1.call-start = ((), (), s32[]{:S(2)}) async-start(), calls=%async_computation.40 | async-start | bytes 3538944
  1540.5 215.1 %reduce-scatter.32.cloned.1.call-start = ((), (), s32[]{:S(2)}) async-start(), calls=%async_computation.39 | async-start | bytes 3538944 | tf_op jit(solution)/shard_map/reduce_scatter | solution.py:305
  1551.8 281.1 %reduce-scatter.30.cloned.1.call-start = ((), (), s32[]{:S(2)}) async-start(), calls=%async_computation.38 | async-start | bytes 3538944 | tf_op jit(solution)/shard_map/reduce_scatter | solution.py:302
  1563.2 368.1 %reduce-scatter.28.cloned.1.call-start = ((), (), s32[]{:S(2)}) async-start(), calls=%async_computation.37 | async-start | bytes 5308416 | tf_op jit(solution)/shard_map/reduce_scatter | solution.py:81
  1570.8 459.5 %reduce-scatter.22.cloned.1.call-start = ((), (), s32[]{:S(2)}) async-start(), calls=%async_computation.34 | async-start | bytes 5308416 | tf_op jit(solution)/shard_map/reduce_scatter | solution.py:72
  1581.9 521.2 %reduce-scatter.24.cloned.1.call-start = ((), (), s32[]{:S(2)}) async-start(), calls=%async_computation.35 | async-start | bytes 2654208 | tf_op jit(solution)/shard_map/reduce_scatter | solution.py:75
  1589.4 585.5 %reduce-scatter.26.cloned.1.call-start = ((), (), s32[]{:S(2)}) async-start(), calls=%async_computation.36 | async-start | bytes 2654208 | tf_op jit(solution)/shard_map/reduce_scatter | solution.py:78
  1603.6 620.0 %all-reduce.14.cloned.1.call-start = ((), (), s32[]{:S(2)}) async-start(), calls=%async_computation.41 | async-start | bytes 3538944 | tf_op jit(solution)/shard_map/psum | solution.py:92
  (73 other events, 1667.4 us)
Sparse Core Ops, SparseCore 0:
  10.2 69.5 all-gather.21
  81.9 81.4 all-gather.25
  165.6 27.0 all-gather.19
  194.7 28.9 all-gather.23
  225.7 79.8 all-gather.27
  307.7 58.5 all-gather.31
  368.4 44.9 all-gather.29
  415.6 60.4 all-gather.33
  478.3 59.0 all-gather.35
  557.7 56.9 reduce-scatter.13
  618.8 69.0 all-gather.43
  690.2 80.4 all-gather.47
  772.9 27.0 all-gather.41
  802.1 28.9 all-gather.45
  833.3 79.8 all-gather.49
  915.5 58.5 all-gather.55
  975.6 44.9 all-gather.51
  1023.0 60.4 all-gather.53
  1085.1 45.0 all-gather.39
  1132.4 60.4 all-gather.37
  1231.7 97.6 reduce-scatter.15
  1521.0 37.9 reduce-scatter.17
  1561.6 37.9 reduce-scatter.19
  1603.4 74.3 reduce-scatter.33
  1681.8 73.7 reduce-scatter.31
  1759.5 73.3 reduce-scatter.29
  1836.9 94.3 reduce-scatter.27
  1935.4 94.9 reduce-scatter.21
  2034.3 68.7 reduce-scatter.23
  2106.8 68.0 reduce-scatter.25
  2177.7 45.7 all-reduce.13
